TPU v7x, 32 devices: a whole 2x2x4 slice. The times are simulated.
32 devices in a mesh: dp: 8 (over z, y), rep: 4 (over x, core).
Axes of the slice: x: 2, y: 2, z: 4, core: 2. Of those that a mesh axis runs over, the one named last changes fastest.
Arguments:
- packet_bytes: int32 [4096, 256], P(('dp', 'rep')), may hold values from 0 to 255
- owner_index: int32 [4096], P(('dp', 'rep')), may hold values from 0 to 7, as said below
- session_id: int32 [4096], P(('dp', 'rep')), may hold values from 0 to 15
- class_label: int32 [512], P(('dp', 'rep')), may hold values from 0 to 127
- byte_table: bfloat16 [256, 64], replicated, may hold values from -6 to 6
- w_conv: bfloat16 [512, 512], replicated, may hold values from -0.25 to 0.25
- norm_gain: bfloat16 [512], replicated, may hold values from 0.099609375 to 1.8984375
- w_project: bfloat16 [512, 1536], replicated, may hold values from -7 to 7
- w_out: bfloat16 [512, 512], replicated, may hold values from -0.25 to 0.25
- w_head: bfloat16 [512, 128], replicated, may hold values from -4 to 4
Outputs:
- logits: float32 [512, 128], P(('dp', 'rep'))
- grad_table: float32 [256, 64], replicated
- grad_conv: float32 [512, 512], replicated
- grad_gain: float32 [512], replicated
- grad_project: float32 [512, 1536], replicated
- grad_out: float32 [512, 512], replicated
- grad_head: float32 [512, 128], replicated
Inputs may be any that keep to these rules, and one draw needn't show every extreme that they name: `owner_index`: of one device's packets at most 32 name any one owner; in each group along dp one owner is named by exactly 32 packets of every device of the group.
All inputs are finite; a program needn't handle non-finite values.
Results may differ from a plain program's by a relative error of at most 0.01.
Values may be sent and summed in bfloat16 or wider, within the bound.
No kernel may reach another device: no remote copies, remote signals or barrier semaphores. Data moves between devices by JAX's collectives and lax.ppermute only.
A program may use at most 128 MiB of HBM per device.

v0:
```python
import jax
import jax.numpy as jnp
from jax import lax
from jax.sharding import PartitionSpec as P

BYTES = 256
KERNEL = 8
HEADS = 8
SESS = 16
NORM_EPS = 1e-06


def silu_slope(values_in):
    sigma = jax.nn.sigmoid(values_in)
    return sigma * (1.0 + values_in * (1.0 - sigma))


def lookup_block(block_codes, byte_table):
    vocab = lax.broadcasted_iota(jnp.int32, (1, 1, 256), 2)
    onehot = (block_codes[:, :, None] == vocab).astype(jnp.bfloat16)
    return jnp.einsum("pbv,vc->pbc", onehot, byte_table, preferred_element_type=jnp.float32).astype(
        jnp.bfloat16
    )


def windows_of(byte_codes, byte_table):
    packets, length = byte_codes.shape
    blocks = byte_codes.reshape(packets // 16, 16, length)
    feats = lax.map(lambda block_codes: lookup_block(block_codes, byte_table), blocks)
    return feats.reshape(packets, length // KERNEL, KERNEL * byte_table.shape[1])


def session_layer(received, recv_session, labels_here, norm_gain, w_project, w_out, w_head):
    f32 = jnp.float32
    bf16 = jnp.bfloat16
    slot_count, model_width = received.shape
    head_dim = model_width // HEADS
    score_scale = head_dim ** (-0.5)
    as_float = received.astype(f32)
    inverse = lax.rsqrt(jnp.mean(as_float * as_float, axis=1, keepdims=True) + NORM_EPS)
    gain_f = norm_gain.astype(f32)
    norm_in = (as_float * inverse * gain_f).astype(bf16)
    projected = jnp.dot(norm_in, w_project, preferred_element_type=f32).astype(bf16)
    projected = projected.reshape(slot_count, 3, HEADS, head_dim)
    queries = projected[:, 0]
    keys_all = projected[:, 1]
    values = projected[:, 2]
    same_session = recv_session[:, None] == recv_session[None, :]
    scores = jnp.einsum("qhd,khd->hqk", queries, keys_all, preferred_element_type=f32) * score_scale
    scores = jnp.where(same_session[None], scores, -1e30)
    row_max = jnp.max(scores, axis=2, keepdims=True)
    shifted = jnp.exp(scores - row_max)
    mixing = shifted / jnp.sum(shifted, axis=2, keepdims=True)
    mixing_b = mixing.astype(bf16)
    attended = jnp.einsum("hqk,khd->qhd", mixing_b, values, preferred_element_type=f32).astype(bf16)
    attended = attended.reshape(slot_count, model_width)
    hidden = as_float + jnp.dot(attended, w_out, preferred_element_type=f32)
    member = (recv_session[None, :] == lax.broadcasted_iota(jnp.int32, (SESS, 1), 0)).astype(f32)
    counts = jnp.maximum(jnp.sum(member, axis=1, keepdims=True), 1.0)
    pooled = jnp.dot(member, hidden, precision=lax.Precision.HIGHEST) / counts
    pooled_b = pooled.astype(bf16)
    logits = jnp.dot(pooled_b, w_head, preferred_element_type=f32)
    class_probs = jax.nn.softmax(logits, axis=1)
    target = (
        labels_here[:, None] == lax.broadcasted_iota(jnp.int32, (1, w_head.shape[1]), 1)
    ).astype(f32)
    dlogits = (class_probs - target) / SESS
    grad_head = jnp.dot(pooled_b.astype(f32).T, dlogits, precision=lax.Precision.HIGHEST)
    dpooled = jnp.dot(dlogits, w_head.astype(f32).T, precision=lax.Precision.HIGHEST)
    dhidden = jnp.dot(member.T, dpooled / counts, precision=lax.Precision.HIGHEST)
    dhidden_b = dhidden.astype(bf16)
    grad_out = jnp.einsum("rk,rd->kd", attended, dhidden_b, preferred_element_type=f32)
    dattended = jnp.einsum("rd,kd->rk", dhidden_b, w_out, preferred_element_type=f32).astype(bf16)
    dattended = dattended.reshape(slot_count, HEADS, head_dim)
    dmixing = jnp.einsum("qhd,khd->hqk", dattended, values, preferred_element_type=f32)
    dvalues = jnp.einsum("hqk,qhd->khd", mixing_b, dattended, preferred_element_type=f32)
    dscores = (
        mixing * (dmixing - jnp.sum(mixing * dmixing, axis=2, keepdims=True)) * score_scale
    ).astype(bf16)
    dqueries = jnp.einsum("hqk,khd->qhd", dscores, keys_all, preferred_element_type=f32)
    dkeys = jnp.einsum("hqk,qhd->khd", dscores, queries, preferred_element_type=f32)
    dprojected = (
        jnp.stack([dqueries, dkeys, dvalues], axis=1)
        .reshape(slot_count, 3 * model_width)
        .astype(bf16)
    )
    grad_project = jnp.einsum("rk,rd->kd", norm_in, dprojected, preferred_element_type=f32)
    dnorm = jnp.einsum("rd,kd->rk", dprojected, w_project, preferred_element_type=f32)
    grad_gain = jnp.sum(dnorm * as_float * inverse, axis=0)
    scaled = dnorm * gain_f
    d_input = (
        inverse * scaled
        - as_float
        * (inverse * inverse * inverse)
        * jnp.mean(as_float * scaled, axis=1, keepdims=True)
        + dhidden
    )
    return (logits, d_input.astype(bf16), (grad_gain, grad_project, grad_out, grad_head))


def body(
    packet_bytes,
    owner_index,
    session_id,
    class_label,
    byte_table,
    w_conv,
    norm_gain,
    w_project,
    w_out,
    w_head,
):
    f32 = jnp.float32
    bf16 = jnp.bfloat16
    groups = lax.axis_size("dp")
    packet_count = packet_bytes.shape[0]
    slot_count = 2 * packet_count
    capacity = slot_count // groups
    positions = BYTES // KERNEL
    window_width = w_conv.shape[0]
    model_width = w_conv.shape[1]
    windows = windows_of(packet_bytes, byte_table).reshape(-1, window_width)
    conv = jnp.dot(windows, w_conv, preferred_element_type=f32).reshape(
        packet_count, positions, model_width
    )
    embedding = jnp.mean(jax.nn.silu(conv), axis=1).astype(bf16)
    targets = lax.broadcasted_iota(jnp.int32, (1, groups), 1)
    chosen = (owner_index[:, None] == targets).astype(jnp.int32)
    send_rank = jnp.sum((jnp.cumsum(chosen, axis=0) - 1) * chosen, axis=1)
    send_slot = owner_index * capacity + send_rank
    outgoing = jnp.zeros((slot_count, model_width), bf16).at[send_slot].set(embedding)
    out_session = jnp.full((slot_count,), -1.0, bf16).at[send_slot].set(session_id.astype(bf16))
    incoming, in_session = (
        lax.all_to_all(
            outgoing.reshape(groups, capacity, model_width),
            "dp",
            split_axis=0,
            concat_axis=0,
            tiled=True,
        ),
        lax.all_to_all(
            out_session.reshape(groups, capacity), "dp", split_axis=0, concat_axis=0, tiled=True
        ),
    )
    received = incoming.reshape(slot_count, model_width)
    recv_session = in_session.reshape(slot_count).astype(jnp.int32)
    logits, d_input, owner_grads = session_layer(
        received, recv_session, class_label, norm_gain, w_project, w_out, w_head
    )
    returned = lax.all_to_all(
        d_input.reshape(groups, capacity, model_width),
        "dp",
        split_axis=0,
        concat_axis=0,
        tiled=True,
    )
    dembedding = returned.reshape(slot_count, model_width)[send_slot]
    dconv = (
        (dembedding.astype(f32)[:, None, :] / positions * silu_slope(conv))
        .astype(bf16)
        .reshape(-1, model_width)
    )
    grad_conv = jnp.einsum("rk,rd->kd", windows, dconv, preferred_element_type=f32)
    dwindows = jnp.einsum("rd,kd->rk", dconv, w_conv, preferred_element_type=f32).astype(bf16)
    chan_count = byte_table.shape[1]
    dwindows = dwindows.reshape(packet_count // 16, 16 * BYTES, chan_count)
    code_blocks = packet_bytes.reshape(packet_count // 16, 16 * BYTES)

    def add_block(total, item):
        block_codes, block_grad = item
        onehot = (block_codes[:, None] == lax.broadcasted_iota(jnp.int32, (1, 256), 1)).astype(bf16)
        return (
            total + jnp.einsum("rv,rc->vc", onehot, block_grad, preferred_element_type=f32),
            None,
        )

    grad_table, unused = lax.scan(
        add_block, jnp.zeros((256, chan_count), f32), (code_blocks, dwindows)
    )
    grads = (grad_table, grad_conv, owner_grads[0], owner_grads[1], owner_grads[2], owner_grads[3])
    totals = lax.psum((grads[0], grads[1], grads[2], grads[3], grads[4], grads[5]), ("dp", "rep"))
    return (logits, totals[0], totals[1], totals[2], totals[3], totals[4], totals[5])


def solution(mesh):
    in_specs = (
        P(("dp", "rep"), None),
        P(("dp", "rep")),
        P(("dp", "rep")),
        P(("dp", "rep")),
        P(),
        P(),
        P(),
        P(),
        P(),
        P(),
    )
    out_specs = (P(("dp", "rep"), None), P(), P(), P(), P(), P(), P())
    return jax.shard_map(body, mesh=mesh, in_specs=in_specs, out_specs=out_specs, check_vma=False)
```

profile of v0, /device:TPU:0, one launch (start us, length us, event | category | flops | bytes accessed | tf_op | source)
XLA Modules:
  0.0 378.5 jit_solution(12326877280065003547)
XLA Ops:
  12.4 7.3 %all-to-all-start = ((bf16[8,1,32]{2,1,0:T(2,128)(2,1)}), bf16[8,1,32]{2,1,0:T(2,128)(2,1)S(1)}, u32[]{:S(2)}, u32[]{:S(2)}) async-start(bf16[8,1,32]{2,1,0:T(2,128)(2,1)} %all_to_all.16), calls=%async_computation | async-start | bytes 8192 | tf_op jit(solution)/shard_map/all_to_all | solution.py:141
  19.7 26.4 %while.21 = (s32[]{:T(128)}, bf16[8,16,256,64]{2,3,1,0:T(8,128)(2,1)}, s32[8,16,256]{2,1,0:T(8,128)}, bf16[256,64]{0,1:T(8,128)(2,1)}, s32[]{:T(128)}) while((s32[]{:T(128)}, bf16[8,16,256,64]{2,3,1,0:T(8,128)(2,1)}, s32[8,16,256]{2,1,0:T(8,128)}, bf16[256,64]{0,1:T(8,128)(2,1)}, s32[]{:T(128)}) %tuple.55), condition=%wide.region_4.5_spmd, body=%wide.region_3.4_spmd.sunk | while | flops 135528448 | bytes 606285 | solution.py:29
  46.1 8.5 %copy.48 = bf16[8,16,256,64]{3,2,1,0:T(8,128)(2,1)} copy(bf16[8,16,256,64]{2,3,1,0:T(8,128)(2,1)} %get-tuple-element.51) | data formatting | bytes 8388608 | tf_op jit(solution)/shard_map/while | solution.py:29
  54.6 11.8 %dot_general.68 = bf16[128,32,512]{2,1,0:T(8,128)(2,1)} reshape(bf16[8,16,256,64]{3,2,1,0:T(8,128)(2,1)} %copy.48) | data formatting | bytes 8388608 | tf_op jit(solution)/shard_map/dot_general | solution.py:123
  66.4 14.6 %multiply_reduce_fusion = (f32[128,512]{1,0:T(8,128)S(1)}, f32[128,32,512]{2,0,1:T(8,128)}) fusion(bf16[512,512]{1,0:T(8,128)(2,1)S(1)} %copy-done.29, bf16[128,32,512]{2,1,0:T(8,128)(2,1)} %dot_general.68), kind=kOutput, calls=%fused_computation.22 | convolution fusion | flops 2157903872 | bytes 13369344 | tf_op jit(solution)/shard_map/dot_general | solution.py:123
  81.6 11.8 %reshape_reshape.3 = bf16[4096,512]{1,0:T(8,128)(2,1)} reshape(bf16[8,16,256,64]{3,2,1,0:T(8,128)(2,1)} %copy.48) | data formatting | bytes 8388608 | tf_op jit(solution)/shard_map/reshape;reshape | solution.py:122
  95.1 6.0 %all-to-all-start.1 = ((bf16[8,32,512]{2,1,0:T(8,128)(2,1)}), bf16[8,32,512]{2,1,0:T(8,128)(2,1)S(1)}, u32[]{:S(2)}, u32[]{:S(2)}) async-start(bf16[8,32,512]{2,1,0:T(8,128)(2,1)} %bitcast.5), calls=%async_computation.1 | async-start | bytes 524288 | tf_op jit(solution)/shard_map/all_to_all | solution.py:134
  102.6 7.0 %all-to-all-done.1 = bf16[8,32,512]{2,1,0:T(8,128)(2,1)S(1)} async-done(((bf16[8,32,512]{2,1,0:T(8,128)(2,1)}), bf16[8,32,512]{2,1,0:T(8,128)(2,1)S(1)}, u32[]{:S(2)}, u32[]{:S(2)}) %all-to-all-start.1) | async-done | bytes 262176 | tf_op jit(solution)/shard_map/all_to_all | solution.py:134
  126.8 5.0 %fusion.26 = bf16[256,1,8,64]{0,3,2,1:T(8,128)(2,1)} fusion(f32[8,256,256]{1,2,0:T(8,128)} %fusion.53, bf16[256,3,8,64]{0,3,2,1:T(8,128)(2,1)S(1)} %bitcast.141, f32[8,256,256]{1,2,0:T(8,128)} %get-tuple-element.94, f32[8,256]{1,0:T(8,128)} %copy-done.31), kind=kOutput, calls=%fused_computation.37 | convolution fusion | flops 70781184 | bytes 8929280 | tf_op jit(solution)/shard_map/hqk,khd->qhd/dot_general | solution.py:80
  131.8 5.0 %fusion.29 = bf16[256,1,8,64]{0,3,2,1:T(8,128)(2,1)} fusion(f32[8,256,256]{1,2,0:T(8,128)} %fusion.53, bf16[256,3,8,64]{0,3,2,1:T(8,128)(2,1)S(1)} %bitcast.142, f32[8,256,256]{1,2,0:T(8,128)} %get-tuple-element.94, f32[8,256]{1,0:T(8,128)S(1)} %copy-done.32), kind=kOutput, calls=%fused_computation.38 | convolution fusion | flops 70781184 | bytes 8929280 | tf_op jit(solution)/shard_map/hqk,qhd->khd/dot_general | solution.py:81
  147.7 4.7 %all-to-all-done.2 = bf16[8,32,512]{2,1,0:T(8,128)(2,1)S(1)} async-done(((bf16[8,32,512]{2,1,0:T(8,128)(2,1)}), bf16[8,32,512]{2,1,0:T(8,128)(2,1)S(1)}, u32[]{:S(2)}, u32[]{:S(2)}) %all-to-all-start.2) | async-done | bytes 262176 | tf_op jit(solution)/shard_map/all_to_all | solution.py:150
  153.5 5.0 %multiply_convert_fusion = bf16[128,32,512]{2,0,1:T(8,128)(2,1)S(1)} fusion(f32[128,32,512]{2,0,1:T(8,128)} %get-tuple-element.92, f32[128,512]{1,0:T(8,128)S(1)} %convert_multiply_fusion.2), kind=kLoop, calls=%fused_computation.21 | loop fusion | flops 18874368 | bytes 12845056 | tf_op jit(solution)/shard_map/convert_element_type | solution.py:160
  160.9 4.4 %convolution_convert_fusion = bf16[4096,512]{1,0:T(8,128)(2,1)} fusion(bf16[4096,512]{1,0:T(8,128)(2,1)S(1)} %bitcast.132, bf16[512,512]{1,0:T(8,128)(2,1)S(1)} %copy-done.30), kind=kOutput, calls=%fused_computation.24 | convolution fusion | flops 2149580800 | bytes 8912896 | tf_op jit(solution)/shard_map/rd,kd->rk/dot_general | solution.py:164
  168.6 11.2 %reshape.174 = bf16[8,4096,64]{2,1,0:T(8,128)(2,1)} reshape(bf16[4096,512]{1,0:T(8,128)(2,1)} %convolution_convert_fusion) | data formatting | bytes 8388608 | tf_op jit(solution)/shard_map/reshape | solution.py:166
  179.8 29.5 %while.22 = (s32[]{:T(128)}, f32[256,64]{0,1:T(8,128)S(1)}, s32[8,4096]{1,0:T(8,128)S(1)}, bf16[8,4096,64]{2,1,0:T(8,128)(2,1)}, s32[]{:T(128)}, /*index=5*/s32[]{:T(128)}) while((s32[]{:T(128)}, f32[256,64]{0,1:T(8,128)S(1)}, s32[8,4096]{1,0:T(8,128)S(1)}, bf16[8,4096,64]{2,1,0:T(8,128)(2,1)}, s32[]{:T(128)}, ...), condition=%wide.region_16.17_spmd.clone, body=%wide.region_15.16_spmd.clone.sunk | while | flops 135299072 | bytes 1228895 | solution.py:177
  179.8 3.6 fusion.108
  183.5 3.6 fusion.108
  187.2 3.6 fusion.108
  190.9 3.6 fusion.108
  194.6 3.6 fusion.108
  198.2 3.6 fusion.108
  209.9 39.5 %psum.44 = f32[512]{0:T(512)} all-reduce(f32[512]{0:T(512)S(1)} %get-tuple-element.68), channel_id=1, replica_groups=mesh['dp'=8,'rep'=4] {'dp','rep'}, use_global_device_ids=true, to_apply=%region_20.21 | all-reduce | flops 512 | bytes 4096 | tf_op jit(solution)/shard_map/psum | solution.py:181
  249.5 112.7 %all-reduce.3.cloned.1.call-done = (f32[256,64]{0,1:T(8,128)}, f32[512,512]{1,0:T(8,128)}, f32[512,1536]{1,0:T(8,128)}, f32[512,512]{1,0:T(8,128)}, f32[512,128]{1,0:T(8,128)}) async-done(((f32[256,64]{0,1:T(8,128)}, f32[512,512]{1,0:T(8,128)}, f32[512,1536]{1,0:T(8,128)}, f32[512,512]{1,0:T(8,128)}, f32[512,128]{1,0:T(8,128)}), (f32[256,64]{0,1:T(8,128)}, f32[512,512]{1,0:T(8,128)}, f32[512,1536]{1,0:T(8,128)}, ...) | async-done | bytes 5570576 | tf_op jit(solution)/shard_map/psum | solution.py:181
  365.9 3.9 %copy.86 = f32[512,1536]{1,0:T(8,128)} copy(f32[512,1536]{1,0:T(8,128)} %get-tuple-element.187) | data formatting | bytes 6291456
  (148 shorter events, 83.5 us)
Async XLA Ops:
  7.2 103.9 %copy-start = (bf16[512,1536]{1,0:T(8,128)(2,1)S(1)}, bf16[512,1536]{1,0:T(8,128)(2,1)}, u32[]{:S(2)}) copy-start(bf16[512,1536]{1,0:T(8,128)(2,1)} %param.21) | copy-start | bytes 4718596
  12.4 82.7 %all-to-all-start = ((bf16[8,1,32]{2,1,0:T(2,128)(2,1)}), bf16[8,1,32]{2,1,0:T(2,128)(2,1)S(1)}, u32[]{:S(2)}, u32[]{:S(2)}) async-start(bf16[8,1,32]{2,1,0:T(2,128)(2,1)} %all_to_all.16), calls=%async_computation | async-start | bytes 8192 | tf_op jit(solution)/shard_map/all_to_all | solution.py:141
  54.6 11.8 %copy-start.29 = (bf16[512,512]{1,0:T(8,128)(2,1)S(1)}, bf16[512,512]{1,0:T(8,128)(2,1)}, u32[]{:S(2)}) copy-start(bf16[512,512]{1,0:T(8,128)(2,1)} %param.19) | copy-start | bytes 1572868
  66.4 15.2 %copy-start.6 = (s32[8,16,256]{2,1,0:T(8,128)S(1)}, s32[8,16,256]{2,1,0:T(8,128)}, u32[]{:S(2)}) copy-start(s32[8,16,256]{2,1,0:T(8,128)} %get-tuple-element.211) | copy-start | bytes 393220
  81.6 11.8 %copy-start.25 = (bf16[512]{0:T(512)(128)(2,1)S(1)}, bf16[512]{0:T(512)(128)(2,1)}, u32[]{:S(2)}) copy-start(bf16[512]{0:T(512)(128)(2,1)} %param.20) | copy-start | bytes 3076
  93.4 16.5 %copy-start.15 = (f32[512]{0:T(512)}, f32[512]{0:T(512)S(1)}, u32[]{:S(2)}) copy-start(f32[512]{0:T(512)S(1)} %convert_element_type.118) | copy-start | bytes 6148
  95.1 14.5 %all-to-all-start.1 = ((bf16[8,32,512]{2,1,0:T(8,128)(2,1)}), bf16[8,32,512]{2,1,0:T(8,128)(2,1)S(1)}, u32[]{:S(2)}, u32[]{:S(2)}) async-start(bf16[8,32,512]{2,1,0:T(8,128)(2,1)} %bitcast.5), calls=%async_computation.1 | async-start | bytes 524288 | tf_op jit(solution)/shard_map/all_to_all | solution.py:134
  101.2 8.4 %copy-start.17 = (s32[256]{0:T(256)}, s32[256]{0:T(256)S(1)}, u32[]{:S(2)}) copy-start(s32[256]{0:T(256)S(1)} %reshape.175) | copy-start | bytes 3076
  115.0 2.3 copy-start.18
  115.0 2.4 copy-start.28
  122.1 2.8 copy-start.4
  126.8 5.0 %copy-start.32 = (f32[8,256]{1,0:T(8,128)S(1)}, f32[8,256]{1,0:T(8,128)}, u32[]{:S(2)}) copy-start(f32[8,256]{1,0:T(8,128)} %copy-done.31) | copy-start | bytes 24580
  138.0 6.2 %copy-start.14 = (f32[8,32]{1,0:T(8,128)S(1)}, f32[8,32]{1,0:T(8,128)}, u32[]{:S(2)}) copy-start(f32[8,32]{1,0:T(8,128)} %copy-done.13) | copy-start | bytes 3076
  139.5 4.8 %copy-start.10 = (f32[16,128]{1,0:T(8,128)S(1)}, f32[16,128]{1,0:T(8,128)}, u32[]{:S(2)}) copy-start(f32[16,128]{1,0:T(8,128)} %copy-done.9) | copy-start | bytes 24580
  139.5 4.8 %copy-start.22 = (f32[16]{0:T(128)S(1)}, f32[16]{0:T(128)}, u32[]{:S(2)}) copy-start(f32[16]{0:T(128)} %copy-done.21) | copy-start | bytes 196
  139.6 4.8 %copy-start.24 = (f32[16]{0:T(128)S(1)}, f32[16]{0:T(128)}, u32[]{:S(2)}) copy-start(f32[16]{0:T(128)} %copy-done.23) | copy-start | bytes 196
  139.6 4.8 %copy-start.27 = (s32[16]{0:T(128)S(1)}, s32[16]{0:T(128)}, u32[]{:S(2)}) copy-start(s32[16]{0:T(128)} %param.17) | copy-start | bytes 196
  140.5 12.0 %all-to-all-start.2 = ((bf16[8,32,512]{2,1,0:T(8,128)(2,1)}), bf16[8,32,512]{2,1,0:T(8,128)(2,1)S(1)}, u32[]{:S(2)}, u32[]{:S(2)}) async-start(bf16[8,32,512]{2,1,0:T(8,128)(2,1)} %bitcast.21), calls=%async_computation.2 | async-start | bytes 524288 | tf_op jit(solution)/shard_map/all_to_all | solution.py:150
  143.9 218.2 %all-reduce.3.cloned.1.call-start = ((), (), s32[]{:S(2)}) async-start(), calls=%async_computation.3 | async-start | bytes 11141120 | tf_op jit(solution)/shard_map/psum | solution.py:181
  158.5 2.4 copy-start.30
  160.9 4.4 %copy-start.2 = (bf16[4096,512]{1,0:T(8,128)(2,1)S(1)}, bf16[4096,512]{1,0:T(8,128)(2,1)}, u32[]{:S(2)}) copy-start(bf16[4096,512]{1,0:T(8,128)(2,1)} %reshape_reshape.3) | copy-start | bytes 12582916
  168.6 11.2 %copy-start.11 = (f32[256,64]{0,1:T(8,128)S(1)}, f32[256,64]{0,1:T(8,128)}, u32[]{:S(2)}) copy-start(f32[256,64]{0,1:T(8,128)} %custom-call) | copy-start | bytes 196612
  365.9 3.9 %copy-start.5 = (f32[512,512]{1,0:T(8,128)S(1)}, f32[512,512]{1,0:T(8,128)}, u32[]{:S(2)}) copy-start(f32[512,512]{1,0:T(8,128)} %get-tuple-element.188) | copy-start | bytes 3145732
  365.9 5.7 %copy-start.1 = (bf16[512,1536]{1,0:T(8,128)(2,1)S(1)}, bf16[512,1536]{1,0:T(8,128)(2,1)}, u32[]{:S(2)}) copy-start(bf16[512,1536]{1,0:T(8,128)(2,1)} %param.21) | copy-start | bytes 4718596
  (13 other events, 14.7 us)
Sparse Core Ops, SparseCore 0:
  210.1 152.0 all-reduce.2
where the time goes:
time: 382 us; the launch traced here: 378 us
  waiting for transfers between devices  125 us (33%)
  matrix products  100 us (26%)
  local copies, waits for them, and re-layouts  68 us (18%)
  blocking collectives  39.5 us (10%)
  starting transfers between devices  17 us (4%)
  other arithmetic  14.6 us (4%)
  between operations  14.5 us (4%)
    psum x1, waiting for transfers between devices, body(): lax.psum((grads[0], grads[1], grads[2], grads[3], grads[4], grads[5]), ('...  113 us
    psum x1, blocking collectives, body(): lax.psum((grads[0], grads[1], grads[2], grads[3], grads[4], grads[5]), ('...  39.5 us
    dot_general x8, matrix products, add_block(): jnp.einsum('rv,rc->vc', onehot, block_grad, preferred_element_type=f32)  29.1 us
    dot_general x8, matrix products, lookup_block(): jnp.einsum('pbv,vc->pbc', onehot, byte_table, preferred_element_type=jnp....  20.6 us
    dot_general x1, matrix products, body(): jnp.dot(windows, w_conv, preferred_element_type=f32)  14.6 us
    unnamed x71, local copies, waits for them, and re-layouts  12.2 us
    dot_general x1, local copies, waits for them, and re-layouts, body(): jnp.dot(windows, w_conv, preferred_element_type=f32)  11.8 us
    another operation x1, local copies, waits for them, and re-layouts, body(): windows = windows_of(packet_bytes, byte_table).reshape(-1, window_width)  11.8 us
  transfers between devices with their start and end apart: 4, of which 3 were waited for; matrix products, arithmetic and copies ran while one was open for 21% of the time, Pallas kernels for 0%

commit v1 on v0

--- a/solution.py
+++ b/solution.py
@@ -178,7 +178,8 @@
         add_block, jnp.zeros((256, chan_count), f32), (code_blocks, dwindows)
     )
     grads = (grad_table, grad_conv, owner_grads[0], owner_grads[1], owner_grads[2], owner_grads[3])
-    totals = lax.psum((grads[0], grads[1], grads[2], grads[3], grads[4], grads[5]), ("dp", "rep"))
+    half = lax.psum((grads[0], grads[1], grads[2], grads[3], grads[4], grads[5]), "rep")
+    totals = lax.psum(half, "dp")
     return (logits, totals[0], totals[1], totals[2], totals[3], totals[4], totals[5])
 
 

time: 382 us -> 536 us (1.40)
  waiting for transfers between devices: 125 us -> 290 us
  blocking collectives: 39.5 us -> 28.7 us
    psum x1 -> x2, waiting for transfers between devices: 113 us -> 279 us  [the longest x1 171 us: body(): totals = lax.psum(half, 'dp')]
    psum x1 -> x2, blocking collectives: 39.5 us -> 28.7 us  [the longest x1 22.8 us: body(): totals = lax.psum(half, 'dp')]
    unnamed x71 -> x73, local copies, waits for them, and re-layouts: 12.2 us -> 11.2 us
  transfers between devices with their start and end apart: 4 -> 5, of which waited for: 3 -> 4; matrix products, arithmetic and copies ran while one was open for 21% -> 15% of each run, Pallas kernels for 0% -> 0%
where the time goes in v1:
time: 536 us; the launch traced here: 533 us
  waiting for transfers between devices  290 us (54%)
  matrix products  100 us (19%)
  local copies, waits for them, and re-layouts  67 us (12%)
  blocking collectives  28.7 us (5%)
  starting transfers between devices  17 us (3%)
  other arithmetic  15.1 us (3%)
  between operations  14.5 us (3%)
    psum x1, waiting for transfers between devices, body(): totals = lax.psum(half, 'dp')  171 us
    psum x1, waiting for transfers between devices, body(): lax.psum((grads[0], grads[1], grads[2], grads[3], grads[4], grads[5]), 'r...  108 us
    dot_general x8, matrix products, add_block(): jnp.einsum('rv,rc->vc', onehot, block_grad, preferred_element_type=f32)  29.1 us
    psum x1, blocking collectives, body(): totals = lax.psum(half, 'dp')  22.8 us
    dot_general x8, matrix products, lookup_block(): jnp.einsum('pbv,vc->pbc', onehot, byte_table, preferred_element_type=jnp....  20.6 us
    dot_general x1, matrix products, body(): jnp.dot(windows, w_conv, preferred_element_type=f32)  14.6 us
    dot_general x1, local copies, waits for them, and re-layouts, body(): jnp.dot(windows, w_conv, preferred_element_type=f32)  11.8 us
    another operation x1, local copies, waits for them, and re-layouts, body(): windows = windows_of(packet_bytes, byte_table).reshape(-1, window_width)  11.8 us
  transfers between devices with their start and end apart: 5, of which 4 were waited for; matrix products, arithmetic and copies ran while one was open for 15% of the time, Pallas kernels for 0%

profile of v1, /device:TPU:0, one launch (start us, length us, event | category | flops | bytes accessed | tf_op | source)
XLA Modules:
  0.0 533.1 jit_solution(7274601019604218645)
XLA Ops:
  12.4 7.3 %all-to-all-start = ((bf16[8,1,32]{2,1,0:T(2,128)(2,1)}), bf16[8,1,32]{2,1,0:T(2,128)(2,1)S(1)}, u32[]{:S(2)}, u32[]{:S(2)}) async-start(bf16[8,1,32]{2,1,0:T(2,128)(2,1)} %all_to_all.16), calls=%async_computation | async-start | bytes 8192 | tf_op jit(solution)/shard_map/all_to_all | solution.py:141
  19.7 26.4 %while.21 = (s32[]{:T(128)}, bf16[8,16,256,64]{2,3,1,0:T(8,128)(2,1)}, s32[8,16,256]{2,1,0:T(8,128)}, bf16[256,64]{0,1:T(8,128)(2,1)}, s32[]{:T(128)}) while((s32[]{:T(128)}, bf16[8,16,256,64]{2,3,1,0:T(8,128)(2,1)}, s32[8,16,256]{2,1,0:T(8,128)}, bf16[256,64]{0,1:T(8,128)(2,1)}, s32[]{:T(128)}) %tuple.57), condition=%wide.region_4.5_spmd, body=%wide.region_3.4_spmd.sunk | while | flops 135528448 | bytes 606285 | solution.py:29
  46.1 8.5 %copy.48 = bf16[8,16,256,64]{3,2,1,0:T(8,128)(2,1)} copy(bf16[8,16,256,64]{2,3,1,0:T(8,128)(2,1)} %get-tuple-element.51) | data formatting | bytes 8388608 | tf_op jit(solution)/shard_map/while | solution.py:29
  54.6 11.8 %dot_general.68 = bf16[128,32,512]{2,1,0:T(8,128)(2,1)} reshape(bf16[8,16,256,64]{3,2,1,0:T(8,128)(2,1)} %copy.48) | data formatting | bytes 8388608 | tf_op jit(solution)/shard_map/dot_general | solution.py:123
  66.4 14.6 %multiply_reduce_fusion = (f32[128,512]{1,0:T(8,128)S(1)}, f32[128,32,512]{2,0,1:T(8,128)}) fusion(bf16[512,512]{1,0:T(8,128)(2,1)S(1)} %copy-done.30, bf16[128,32,512]{2,1,0:T(8,128)(2,1)} %dot_general.68), kind=kOutput, calls=%fused_computation.22 | convolution fusion | flops 2157903872 | bytes 13369344 | tf_op jit(solution)/shard_map/dot_general | solution.py:123
  81.6 11.8 %reshape_reshape.3 = bf16[4096,512]{1,0:T(8,128)(2,1)} reshape(bf16[8,16,256,64]{3,2,1,0:T(8,128)(2,1)} %copy.48) | data formatting | bytes 8388608 | tf_op jit(solution)/shard_map/reshape;reshape | solution.py:122
  95.1 6.0 %all-to-all-start.1 = ((bf16[8,32,512]{2,1,0:T(8,128)(2,1)}), bf16[8,32,512]{2,1,0:T(8,128)(2,1)S(1)}, u32[]{:S(2)}, u32[]{:S(2)}) async-start(bf16[8,32,512]{2,1,0:T(8,128)(2,1)} %bitcast.5), calls=%async_computation.1 | async-start | bytes 524288 | tf_op jit(solution)/shard_map/all_to_all | solution.py:134
  102.6 7.0 %all-to-all-done.1 = bf16[8,32,512]{2,1,0:T(8,128)(2,1)S(1)} async-done(((bf16[8,32,512]{2,1,0:T(8,128)(2,1)}), bf16[8,32,512]{2,1,0:T(8,128)(2,1)S(1)}, u32[]{:S(2)}, u32[]{:S(2)}) %all-to-all-start.1) | async-done | bytes 262176 | tf_op jit(solution)/shard_map/all_to_all | solution.py:134
  126.3 5.0 fusion.26
  131.3 5.0 fusion.29
  147.2 4.7 all-to-all-done.2
  152.9 5.0 multiply_convert_fusion
  160.3 4.4 convolution_convert_fusion
  168.0 11.2 %reshape.174 = bf16[8,4096,64]{2,1,0:T(8,128)(2,1)} reshape(bf16[4096,512]{1,0:T(8,128)(2,1)} %convolution_convert_fusion) | data formatting | bytes 8388608 | tf_op jit(solution)/shard_map/reshape | solution.py:166
  179.2 29.5 %while.22 = (s32[]{:T(128)}, f32[256,64]{0,1:T(8,128)S(1)}, s32[8,4096]{1,0:T(8,128)S(1)}, bf16[8,4096,64]{2,1,0:T(8,128)(2,1)}, s32[]{:T(128)}, /*index=5*/s32[]{:T(128)}) while((s32[]{:T(128)}, f32[256,64]{0,1:T(8,128)S(1)}, s32[8,4096]{1,0:T(8,128)S(1)}, bf16[8,4096,64]{2,1,0:T(8,128)(2,1)}, s32[]{:T(128)}, ...), condition=%wide.region_16.17_spmd.clone, body=%wide.region_15.16_spmd.clone.sunk | while | flops 135299072 | bytes 1228895 | solution.py:177
  186.6 3.6 fusion.108
  190.3 3.6 fusion.108
  197.7 3.6 fusion.108
  201.4 3.6 fusion.108
  209.4 107.6 %all-reduce.7.cloned.1.call-done = (f32[256,64]{0,1:T(8,128)}, f32[512,512]{1,0:T(8,128)}, f32[512,1536]{1,0:T(8,128)}, f32[512,512]{1,0:T(8,128)}, f32[512,128]{1,0:T(8,128)}) async-done(((f32[256,64]{0,1:T(8,128)}, f32[512,512]{1,0:T(8,128)}, f32[512,1536]{1,0:T(8,128)}, f32[512,512]{1,0:T(8,128)}, f32[512,128]{1,0:T(8,128)}), (f32[256,64]{0,1:T(8,128)}, f32[512,512]{1,0:T(8,128)}, f32[512,1536]{1,0:T(8,128)}, ...) | async-done | bytes 5570576 | tf_op jit(solution)/shard_map/psum | solution.py:181
  317.1 5.9 %psum.88 = f32[512]{0:T(512)S(1)} all-reduce(f32[512]{0:T(512)S(1)} %get-tuple-element.68), channel_id=1, replica_groups=mesh['dp'=8,'rep'=4] {'rep'}, use_global_device_ids=true, to_apply=%region_22.23 | all-reduce | flops 512 | bytes 4096 | tf_op jit(solution)/shard_map/psum | solution.py:181
  323.0 22.8 %psum.89 = f32[512]{0:T(512)} all-reduce(f32[512]{0:T(512)S(1)} %psum.88), channel_id=1, replica_groups=mesh['dp'=8,'rep'=4] {'dp'}, use_global_device_ids=true, to_apply=%region_23.24 | all-reduce | flops 512 | bytes 4096 | tf_op jit(solution)/shard_map/psum | solution.py:182
  345.8 171.0 %all-reduce.5.cloned.1.call-done = (f32[256,64]{0,1:T(8,128)}, f32[512,512]{1,0:T(8,128)}, f32[512,1536]{1,0:T(8,128)}, f32[512,512]{1,0:T(8,128)}, f32[512,128]{1,0:T(8,128)}) async-done(((f32[256,64]{0,1:T(8,128)}, f32[512,512]{1,0:T(8,128)}, f32[512,1536]{1,0:T(8,128)}, f32[512,512]{1,0:T(8,128)}, f32[512,128]{1,0:T(8,128)}), (f32[256,64]{0,1:T(8,128)}, f32[512,512]{1,0:T(8,128)}, f32[512,1536]{1,0:T(8,128)}, ...) | async-done | bytes 5570576 | tf_op jit(solution)/shard_map/psum | solution.py:182
  520.6 3.9 copy.91
  (155 shorter events, 90.4 us)
Async XLA Ops:
  7.2 103.4 %copy-start = (bf16[512,1536]{1,0:T(8,128)(2,1)S(1)}, bf16[512,1536]{1,0:T(8,128)(2,1)}, u32[]{:S(2)}) copy-start(bf16[512,1536]{1,0:T(8,128)(2,1)} %param.21) | copy-start | bytes 4718596
  12.4 82.7 %all-to-all-start = ((bf16[8,1,32]{2,1,0:T(2,128)(2,1)}), bf16[8,1,32]{2,1,0:T(2,128)(2,1)S(1)}, u32[]{:S(2)}, u32[]{:S(2)}) async-start(bf16[8,1,32]{2,1,0:T(2,128)(2,1)} %all_to_all.16), calls=%async_computation | async-start | bytes 8192 | tf_op jit(solution)/shard_map/all_to_all | solution.py:141
  54.6 11.8 %copy-start.30 = (bf16[512,512]{1,0:T(8,128)(2,1)S(1)}, bf16[512,512]{1,0:T(8,128)(2,1)}, u32[]{:S(2)}) copy-start(bf16[512,512]{1,0:T(8,128)(2,1)} %param.19) | copy-start | bytes 1572868
  66.4 15.2 %copy-start.6 = (s32[8,16,256]{2,1,0:T(8,128)S(1)}, s32[8,16,256]{2,1,0:T(8,128)}, u32[]{:S(2)}) copy-start(s32[8,16,256]{2,1,0:T(8,128)} %get-tuple-element.232) | copy-start | bytes 393220
  81.6 11.8 %copy-start.26 = (bf16[512]{0:T(512)(128)(2,1)S(1)}, bf16[512]{0:T(512)(128)(2,1)}, u32[]{:S(2)}) copy-start(bf16[512]{0:T(512)(128)(2,1)} %param.20) | copy-start | bytes 3076
  93.4 17.0 %copy-start.15 = (f32[512]{0:T(512)}, f32[512]{0:T(512)S(1)}, u32[]{:S(2)}) copy-start(f32[512]{0:T(512)S(1)} %convert_element_type.118) | copy-start | bytes 6148
  95.1 14.5 %all-to-all-start.1 = ((bf16[8,32,512]{2,1,0:T(8,128)(2,1)}), bf16[8,32,512]{2,1,0:T(8,128)(2,1)S(1)}, u32[]{:S(2)}, u32[]{:S(2)}) async-start(bf16[8,32,512]{2,1,0:T(8,128)(2,1)} %bitcast.5), calls=%async_computation.1 | async-start | bytes 524288 | tf_op jit(solution)/shard_map/all_to_all | solution.py:134
  101.2 8.4 %copy-start.17 = (s32[256]{0:T(256)}, s32[256]{0:T(256)S(1)}, u32[]{:S(2)}) copy-start(s32[256]{0:T(256)S(1)} %reshape.175) | copy-start | bytes 3076
  114.5 2.4 copy-start.29
  121.6 2.8 copy-start.4
  126.3 5.0 copy-start.33
  137.5 6.2 %copy-start.14 = (f32[8,32]{1,0:T(8,128)S(1)}, f32[8,32]{1,0:T(8,128)}, u32[]{:S(2)}) copy-start(f32[8,32]{1,0:T(8,128)} %copy-done.13) | copy-start | bytes 3076
  139.0 4.8 copy-start.10
  139.0 4.8 copy-start.22
  139.0 4.8 copy-start.25
  139.0 4.8 copy-start.28
  140.0 12.0 %all-to-all-start.2 = ((bf16[8,32,512]{2,1,0:T(8,128)(2,1)}), bf16[8,32,512]{2,1,0:T(8,128)(2,1)S(1)}, u32[]{:S(2)}, u32[]{:S(2)}) async-start(bf16[8,32,512]{2,1,0:T(8,128)(2,1)} %bitcast.21), calls=%async_computation.2 | async-start | bytes 524288 | tf_op jit(solution)/shard_map/all_to_all | solution.py:150
  143.4 173.6 %all-reduce.7.cloned.1.call-start = ((), (), s32[]{:S(2)}) async-start(), calls=%async_computation.4 | async-start | bytes 11141120 | tf_op jit(solution)/shard_map/psum | solution.py:181
  157.9 2.4 copy-start.31
  160.3 4.4 copy-start.2
  168.0 11.2 %copy-start.11 = (f32[256,64]{0,1:T(8,128)S(1)}, f32[256,64]{0,1:T(8,128)}, u32[]{:S(2)}) copy-start(f32[256,64]{0,1:T(8,128)} %custom-call) | copy-start | bytes 196612
  209.4 307.4 %all-reduce.5.cloned.1.call-start = ((), (), s32[]{:S(2)}) async-start(), calls=%async_computation.3 | async-start | bytes 11141120 | tf_op jit(solution)/shard_map/psum | solution.py:182
  520.5 3.9 copy-start.5
  520.5 5.7 %copy-start.1 = (bf16[512,1536]{1,0:T(8,128)(2,1)S(1)}, bf16[512,1536]{1,0:T(8,128)(2,1)}, u32[]{:S(2)}) copy-start(bf16[512,1536]{1,0:T(8,128)(2,1)} %param.21) | copy-start | bytes 4718596
  (15 other events, 18.7 us)
Sparse Core Ops, SparseCore 0:
  209.5 107.4 all-reduce.6
  321.9 194.8 all-reduce.4
